TPU v7x, 32 devices: a whole 2x2x4 slice. The times are simulated.
32 devices in a mesh: seq: 8 (over z, x), head: 4 (over y, core).
Axes of the slice: x: 2, y: 2, z: 4, core: 2. Of those that a mesh axis runs over, the one named last changes fastest.
Arguments:
- hidden: bfloat16 [8192, 8192], P('seq'), may hold values from -27 to 27, as said below
- key_value_weight: bfloat16 [8192, 2048], P('seq', 'head'), may hold values from -0.0625 to 0.0625
- down_projection: bfloat16 [2048, 512], P('head'), may hold values from -0.125 to 0.125
- up_projection: bfloat16 [512, 2048], P(None, 'head'), may hold values from -0.25 to 0.25
- positions: int32 [8192], P('seq'), may hold values from 0 to 131071
Outputs:
- grad_down: float32 [512, 2048], P('seq', 'head')
- grad_up: float32 [512, 2048], P('seq', 'head')
- rel_error: float32 [], replicated
Inputs may be any that keep to these rules, and one draw needn't show every extreme that they name: `hidden`: real-valued inputs, rows of differing scale.
All inputs are finite; a program needn't handle non-finite values.
Results may differ from a plain program's by a relative error of at most 0.0045.
Values may be sent and summed in bfloat16 or wider, within the bound.
A program may use at most 64 MiB of HBM per device.

v0:
```python
import math
import jax
import jax.numpy as jnp
from jax import lax
from jax.sharding import PartitionSpec as P

KEY_VALUE_HEADS = 8
HEAD_SIZE = 128
THETA = 500000.0


def rotate_targets(dense, positions):
    half_dim = HEAD_SIZE // 2
    freqs = jnp.power(
        jnp.float32(THETA), -(jnp.arange(half_dim, dtype=jnp.float32) * 2.0 / HEAD_SIZE)
    )
    angle = positions.astype(jnp.float32)[:, None] * freqs[None, :]
    cosine = jnp.cos(angle)[:, None, :]
    sine = jnp.sin(angle)[:, None, :]
    shaped = dense.reshape(dense.shape[0], -1, 2, HEAD_SIZE)
    key_part = shaped[:, :, 0, :]
    first = key_part[..., :half_dim]
    second = key_part[..., half_dim:]
    turned = jnp.concatenate(
        [first * cosine - second * sine, second * cosine + first * sine], axis=-1
    )
    joined = jnp.stack([turned, shaped[:, :, 1, :]], axis=2)
    return joined.reshape(dense.shape[0], -1).astype(jnp.bfloat16)


def per_device(hidden, key_value_weight, down_projection, up_projection, positions):
    rows_here = hidden.shape[0]
    total_row_count = lax.axis_size("seq") * rows_here
    entry_items = total_row_count * 2 * KEY_VALUE_HEADS * HEAD_SIZE
    dense = jnp.dot(
        hidden,
        lax.all_gather(key_value_weight, "seq", axis=0, tiled=True),
        preferred_element_type=jnp.float32,
    )
    targets = rotate_targets(dense, positions)
    target_wide = targets.astype(jnp.float32)
    energy_local = jnp.sum(target_wide * target_wide)
    partial_value = jnp.dot(targets, down_projection, preferred_element_type=jnp.float32)
    latent = lax.psum(partial_value, "head").astype(jnp.bfloat16)
    rebuilt = jnp.dot(latent, up_projection, preferred_element_type=jnp.float32)
    residual = target_wide - rebuilt
    misfit_local = jnp.sum(residual * residual)
    latent_wide = latent.astype(jnp.float32)
    up_wide = up_projection.astype(jnp.float32)
    grad_up = lax.dot_general(
        latent_wide,
        residual,
        (((0,), (0,)), ((), ())),
        precision=lax.Precision.HIGHEST,
        preferred_element_type=jnp.float32,
    )
    local_grad = lax.dot_general(
        residual,
        up_wide,
        (((1,), (1,)), ((), ())),
        precision=lax.Precision.HIGHEST,
        preferred_element_type=jnp.float32,
    )
    d_latent = lax.psum(local_grad, "head").astype(jnp.bfloat16)
    grad_down = lax.dot_general(
        d_latent, targets, (((0,), (0,)), ((), ())), preferred_element_type=jnp.float32
    )
    grad_down, grad_up = (
        lax.psum_scatter(grad_down, "seq", scatter_dimension=0, tiled=True),
        lax.psum_scatter(grad_up, "seq", scatter_dimension=0, tiled=True),
    )
    misfit, energy = lax.psum((misfit_local, energy_local), ("seq", "head"))
    rel_error = misfit / energy
    factor = -(entry_items / energy) / math.sqrt(total_row_count)
    grad_down = factor * grad_down
    grad_up = factor * grad_up
    return (grad_down, grad_up, rel_error)


def solution(mesh):
    return jax.shard_map(
        per_device,
        mesh=mesh,
        in_specs=(P("seq", None), P("seq", "head"), P("head", None), P(None, "head"), P("seq")),
        out_specs=(P("seq", "head"), P("seq", "head"), P()),
        check_vma=False,
    )
```

profile of v0, /device:TPU:0, one launch (start us, length us, event | category | flops | bytes accessed | tf_op | source)
XLA Modules:
  0.0 349.6 jit_solution(8485636736758103250)
XLA Ops:
  7.2 0.0 copy-start
  7.2 0.0 all-gather.2.cloned.1.call-start
  7.2 0.7 all-gather.2.cloned.1.call-update
  7.9 0.0 reduce-scatter.5.cloned.1.call-start
  8.0 0.7 convert_element_type.24
  8.7 1.0 multiply_cosine_fusion
  9.7 127.7 %all-gather.2.cloned.1.call-done = bf16[8192,512]{1,0:T(8,128)(2,1)} async-done(((bf16[1024,512]{1,0:T(8,128)(2,1)}), bf16[8192,512]{1,0:T(8,128)(2,1)}) %all-gather.2.cloned.1.call-update) | async-done | bytes 8388624 | tf_op jit(solution)/shard_map/all_gather | solution.py:37
  137.3 17.2 %fusion.5 = f32[1024,512]{0,1:T(8,128)S(1)} fusion(bf16[1024,8192]{1,0:T(8,128)(2,1)} %param.5, bf16[8192,512]{1,0:T(8,128)(2,1)} %all-gather.2.cloned.1.call-done), kind=kOutput, calls=%fused_computation.18 | convolution fusion | flops 8589934592 | bytes 27262976 | tf_op jit(solution)/shard_map/dot_general | solution.py:35
  154.6 0.1 slice.19
  154.7 0.1 slice_bitcast_fusion
  154.8 0.2 multiply_subtract_fusion
  155.0 0.0 copy-start.4
  155.0 1.1 multiply_reduce_fusion.1
  156.2 1.3 copy.10
  157.5 0.0 copy-done.4
  157.5 2.1 fusion.6
  159.6 0.0 copy-done.1
  159.6 41.2 %all-reduce.3 = bf16[1024,512]{1,0:T(8,128)(2,1)} all-reduce(f32[1024,512]{1,0:T(8,128)} %fusion.6), channel_id=1, replica_groups=mesh['seq'=8,'head'=4] {'head'}, use_global_device_ids=true, to_apply=%region_2.0 | all-reduce | flops 524288 | bytes 3145728 | tf_op jit(solution)/shard_map/psum | solution.py:44
  200.8 3.2 multiply_reduce_fusion
  204.0 2.9 fusion.9
  206.9 3.2 fusion.7
  210.1 0.0 reduce-scatter.5.cloned.1.call-update
  210.1 0.0 reduce-scatter.3.cloned.1.call-start
  210.1 42.8 %all-reduce.4 = bf16[1024,512]{1,0:T(8,128)(2,1)S(1)} all-reduce(f32[1024,512]{1,0:T(8,128)} %fusion.7), channel_id=1, replica_groups=mesh['seq'=8,'head'=4] {'head'}, use_global_device_ids=true, to_apply=%region_3.0 | all-reduce | flops 524288 | bytes 3145728 | tf_op jit(solution)/shard_map/psum | solution.py:64
  252.9 0.0 copy-done.2
  252.9 1.7 fusion.8
  254.7 0.0 reduce-scatter.3.cloned.1.call-update
  254.7 38.7 %all-reduce = (f32[]{:T(128)}, f32[]{:T(128)}) all-reduce(f32[]{:T(128)} %get-tuple-element.5, f32[]{:T(128)} %get-tuple-element.11), channel_id=1, replica_groups=mesh['seq'=8,'head'=4] {'seq','head'}, use_global_device_ids=true, to_apply=%region_1.0 | all-reduce | flops 2 | bytes 16 | tf_op jit(solution)/shard_map/psum | solution.py:72
  295.4 0.0 reduce-scatter.5.cloned.1.call-done
  295.4 1.6 broadcast_multiply_fusion
  297.0 43.4 %reduce-scatter.3.cloned.1.call-done = f32[64,512]{1,0:T(8,128)} async-done(((f32[512,512]{1,0:T(8,128)}), f32[64,512]{1,0:T(8,128)}) %reduce-scatter.3.cloned.1.call-update) | async-done | bytes 131088 | tf_op jit(solution)/shard_map/reduce_scatter | solution.py:69
  340.4 1.6 broadcast_multiply_fusion.1
  (7 shorter events, 0.1 us)
Async XLA Ops:
  7.2 193.6 %copy-start = (bf16[512,512]{1,0:T(8,128)(2,1)S(1)}, bf16[512,512]{1,0:T(8,128)(2,1)}, u32[]{:S(2)}) copy-start(bf16[512,512]{1,0:T(8,128)(2,1)} %param.8) | copy-start | bytes 1572868
  7.2 130.2 %all-gather.2.cloned.1.call-start = ((), (), s32[]{:S(2)}) async-start(), calls=%async_computation.2 | async-start | bytes 9437184 | tf_op jit(solution)/shard_map/all_gather | solution.py:37
  7.9 287.5 %reduce-scatter.5.cloned.1.call-start = ((), (), s32[]{:S(2)}) async-start(), calls=%async_computation.4 | async-start | bytes 1179648 | tf_op jit(solution)/shard_map/reduce_scatter | solution.py:70
  155.0 2.5 copy-start.4
  156.2 3.4 copy-start.1
  200.8 3.2 copy-start.3
  210.1 42.8 %copy-start.2 = (bf16[1024,2,2,128]{0,3,2,1:T(8,128)(2,1)S(1)}, bf16[1024,2,2,128]{0,3,2,1:T(8,128)(2,1)}, u32[]{:S(2)}) copy-start(bf16[1024,2,2,128]{0,3,2,1:T(8,128)(2,1)} %copy-done.1) | copy-start | bytes 3145732
  210.1 130.3 %reduce-scatter.3.cloned.1.call-start = ((), (), s32[]{:S(2)}) async-start(), calls=%async_computation.3 | async-start | bytes 1179648 | tf_op jit(solution)/shard_map/reduce_scatter | solution.py:69
Sparse Core Ops, SparseCore 0:
  10.1 127.1 all-gather.1
  210.2 62.9 reduce-scatter.4
  276.6 63.6 reduce-scatter.2
where the time goes:
time: 350 us
  waiting for transfers between devices  172 us (49%)
  blocking collectives  123 us (35%)
  matrix products  30.4 us (9%)
  between operations  17 us (5%)
  other arithmetic  6.19 us (2%)
    all_gather x1, waiting for transfers between devices, per_device(): lax.all_gather(key_value_weight, 'seq', axis=0, tiled=True)  128 us
    reduce_scatter x1, waiting for transfers between devices, per_device(): lax.psum_scatter(grad_down, 'seq', scatter_dimension=0, tiled=True)  43.4 us
    psum x1, blocking collectives, per_device(): d_latent = lax.psum(local_grad, 'head').astype(jnp.bfloat16)  42.8 us
    psum x1, blocking collectives, per_device(): latent = lax.psum(partial_value, 'head').astype(jnp.bfloat16)  41.2 us
    psum x1, blocking collectives, per_device(): misfit, energy = lax.psum((misfit_local, energy_local), ('seq', 'head'))  38.7 us
    dot_general x1, matrix products, per_device(): jnp.dot(hidden, lax.all_gather(key_value_weight, 'seq', axis=0, tiled=Tru...  17.2 us
  transfers between devices with their start and end apart: 3, of which 2 were waited for; matrix products, arithmetic and copies ran while one was open for 1% of the time, Pallas kernels for 0%

commit v1 on v0

--- a/solution.py
+++ b/solution.py
@@ -61,7 +61,7 @@
         precision=lax.Precision.HIGHEST,
         preferred_element_type=jnp.float32,
     )
-    d_latent = lax.psum(local_grad, "head").astype(jnp.bfloat16)
+    d_latent = jnp.sum(lax.all_gather(local_grad, "head"), axis=0).astype(jnp.bfloat16)
     grad_down = lax.dot_general(
         d_latent, targets, (((0,), (0,)), ((), ())), preferred_element_type=jnp.float32
     )

time: 350 us -> 408 us (1.17)
  waiting for transfers between devices: 172 us -> 265 us
  blocking collectives: 123 us -> 81 us
  other arithmetic: 6.19 us -> 10.8 us
    all_gather x0 -> x1, waiting for transfers between devices: none -> 52.6 us  [per_device(): lax.all_gather(local_grad, 'head')]
    psum x1 -> x0, blocking collectives: 42.8 us -> none  [per_device(): d_latent = lax.psum(local_grad, 'head').astype(jnp.bfloat16)]
    reduce_scatter x1, waiting for transfers between devices: 43.4 us -> 64.9 us  [per_device(): lax.psum_scatter(grad_down, 'seq', scatter_dimension=0, tiled=True)]
    reduce_scatter x1, waiting for transfers between devices: 0.02 us -> 19.4 us  [per_device(): lax.psum_scatter(grad_up, 'seq', scatter_dimension=0, tiled=True)]
    reduce_sum x0 -> x1, other arithmetic: none -> 4.65 us  [per_device(): jnp.sum(lax.all_gather(local_grad, 'head'), axis=0).astype(jnp.bfloat16)]
  transfers between devices with their start and end apart: 3 -> 4, of which waited for: 2 -> 4; matrix products, arithmetic and copies ran while one was open for 1% -> 3% of each run, Pallas kernels for 0% -> 0%
where the time goes in v1:
time: 408 us
  waiting for transfers between devices  265 us (65%)
  blocking collectives  81 us (20%)
  matrix products  31.5 us (8%)
  between operations  17 us (4%)
  other arithmetic  10.8 us (3%)
    all_gather x1, waiting for transfers between devices, per_device(): lax.all_gather(key_value_weight, 'seq', axis=0, tiled=True)  128 us
    reduce_scatter x1, waiting for transfers between devices, per_device(): lax.psum_scatter(grad_down, 'seq', scatter_dimension=0, tiled=True)  64.9 us
    all_gather x1, waiting for transfers between devices, per_device(): lax.all_gather(local_grad, 'head')  52.6 us
    psum x1, blocking collectives, per_device(): latent = lax.psum(partial_value, 'head').astype(jnp.bfloat16)  41.2 us
    psum x1, blocking collectives, per_device(): misfit, energy = lax.psum((misfit_local, energy_local), ('seq', 'head'))  39.9 us
    reduce_scatter x1, waiting for transfers between devices, per_device(): lax.psum_scatter(grad_up, 'seq', scatter_dimension=0, tiled=True)  19.4 us
    dot_general x1, matrix products, per_device(): jnp.dot(hidden, lax.all_gather(key_value_weight, 'seq', axis=0, tiled=Tru...  17.2 us
  transfers between devices with their start and end apart: 4, of which 4 were waited for; matrix products, arithmetic and copies ran while one was open for 3% of the time, Pallas kernels for 0%

profile of v1, /device:TPU:0, one launch (start us, length us, event | category | flops | bytes accessed | tf_op | source)
XLA Modules:
  0.0 407.7 jit_solution(559178472293833179)
XLA Ops:
  7.2 0.0 copy-start
  7.2 0.0 all-gather.4.cloned.1.call-start
  7.2 0.7 all-gather.4.cloned.1.call-update
  7.9 0.0 all-gather.6.cloned.1.call-start
  8.0 0.7 convert_element_type.24
  8.7 1.0 multiply_cosine_fusion
  9.7 127.7 %all-gather.4.cloned.1.call-done = bf16[8192,512]{1,0:T(8,128)(2,1)} async-done(((bf16[1024,512]{1,0:T(8,128)(2,1)}), bf16[8192,512]{1,0:T(8,128)(2,1)}) %all-gather.4.cloned.1.call-update) | async-done | bytes 8388624 | tf_op jit(solution)/shard_map/all_gather | solution.py:37
  137.3 17.2 %fusion.5 = f32[1024,512]{0,1:T(8,128)S(1)} fusion(bf16[1024,8192]{1,0:T(8,128)(2,1)} %param.5, bf16[8192,512]{1,0:T(8,128)(2,1)} %all-gather.4.cloned.1.call-done), kind=kOutput, calls=%fused_computation.18 | convolution fusion | flops 8589934592 | bytes 27262976 | tf_op jit(solution)/shard_map/dot_general | solution.py:35
  154.6 0.1 slice_bitcast_fusion
  154.7 0.1 slice.19
  154.8 0.2 multiply_subtract_fusion
  155.0 0.0 copy-start.3
  155.0 1.1 multiply_reduce_fusion.1
  156.2 1.3 copy.10
  157.5 2.1 fusion.6
  159.6 41.2 %all-reduce.2 = bf16[1024,512]{1,0:T(8,128)(2,1)} all-reduce(f32[1024,512]{1,0:T(8,128)} %fusion.6), channel_id=1, replica_groups=mesh['seq'=8,'head'=4] {'head'}, use_global_device_ids=true, to_apply=%region_2.0 | all-reduce | flops 524288 | bytes 3145728 | tf_op jit(solution)/shard_map/psum | solution.py:44
  200.8 3.1 multiply_reduce_fusion
  203.9 3.2 fusion.7
  207.1 0.0 all-gather.6.cloned.1.call-update
  207.1 0.0 reduce-scatter.5.cloned.1.call-start
  207.2 4.1 %fusion.9 = f32[512,512]{1,0:T(8,128)} fusion(bf16[1024,512]{1,0:T(8,128)(2,1)} %all-reduce.2, f32[1024,512]{1,0:T(8,128)S(1)} %get-tuple-element.12), kind=kOutput, calls=%fused_computation.22 | convolution fusion | flops 3221225472 | bytes 4194304 | tf_op jit(solution)/shard_map/dot_general | solution.py:50
  211.3 0.0 reduce-scatter.5.cloned.1.call-update
  211.3 0.2 reduce-scatter.3.cloned.1.call-start
  211.6 52.6 %all-gather.6.cloned.1.call-done = f32[4096,512]{1,0:T(8,128)} async-done(((f32[1024,512]{1,0:T(8,128)}), f32[4096,512]{1,0:T(8,128)}) %all-gather.6.cloned.1.call-update) | async-done | bytes 8388624 | tf_op jit(solution)/shard_map/all_gather | solution.py:64
  264.2 4.7 %reduce_sum.28 = bf16[1024,512]{1,0:T(8,128)(2,1)S(1)} reduce(f32[4,1024,512]{2,1,0:T(8,128)} %bitcast.24, f32[]{:T(128)} %constant.12.clone.1), dimensions={0}, to_apply=%region_3.0 | reduce | flops 1572864 | bytes 9437188 | tf_op jit(solution)/shard_map/reduce_sum | solution.py:64
  268.9 1.7 fusion.8
  270.6 0.0 reduce-scatter.3.cloned.1.call-update
  270.6 39.9 %all-reduce = (f32[]{:T(128)}, f32[]{:T(128)}) all-reduce(f32[]{:T(128)} %get-tuple-element.5, f32[]{:T(128)} %get-tuple-element.11), channel_id=1, replica_groups=mesh['seq'=8,'head'=4] {'seq','head'}, use_global_device_ids=true, to_apply=%region_1.0 | all-reduce | flops 2 | bytes 16 | tf_op jit(solution)/shard_map/psum | solution.py:72
  312.5 19.4 %reduce-scatter.5.cloned.1.call-done = f32[64,512]{1,0:T(8,128)} async-done(((f32[512,512]{1,0:T(8,128)}), f32[64,512]{1,0:T(8,128)}) %reduce-scatter.5.cloned.1.call-update) | async-done | bytes 131088 | tf_op jit(solution)/shard_map/reduce_scatter | solution.py:70
  331.9 1.6 broadcast_multiply_fusion
  333.5 64.9 %reduce-scatter.3.cloned.1.call-done = f32[64,512]{1,0:T(8,128)} async-done(((f32[512,512]{1,0:T(8,128)}), f32[64,512]{1,0:T(8,128)}) %reduce-scatter.3.cloned.1.call-update) | async-done | bytes 131088 | tf_op jit(solution)/shard_map/reduce_scatter | solution.py:69
  398.4 1.6 broadcast_multiply_fusion.1
  (8 shorter events, 0.1 us)
Async XLA Ops:
  7.2 193.6 %copy-start = (bf16[512,512]{1,0:T(8,128)(2,1)S(1)}, bf16[512,512]{1,0:T(8,128)(2,1)}, u32[]{:S(2)}) copy-start(bf16[512,512]{1,0:T(8,128)(2,1)} %param.8) | copy-start | bytes 1572868
  7.2 130.2 %all-gather.4.cloned.1.call-start = ((), (), s32[]{:S(2)}) async-start(), calls=%async_computation.2 | async-start | bytes 9437184 | tf_op jit(solution)/shard_map/all_gather | solution.py:37
  7.9 256.3 %all-gather.6.cloned.1.call-start = ((), (), s32[]{:S(2)}) async-start(), calls=%async_computation.5 | async-start | bytes 10485760 | tf_op jit(solution)/shard_map/all_gather | solution.py:64
  155.0 2.5 copy-start.3
  156.2 3.4 copy-start.1
  207.1 124.8 %reduce-scatter.5.cloned.1.call-start = ((), (), s32[]{:S(2)}) async-start(), calls=%async_computation.4 | async-start | bytes 1179648 | tf_op jit(solution)/shard_map/reduce_scatter | solution.py:70
  211.3 187.1 %reduce-scatter.3.cloned.1.call-start = ((), (), s32[]{:S(2)}) async-start(), calls=%async_computation.3 | async-start | bytes 1179648 | tf_op jit(solution)/shard_map/reduce_scatter | solution.py:69
  264.2 4.7 %copy-start.2 = (bf16[1024,2,2,128]{0,3,2,1:T(8,128)(2,1)S(1)}, bf16[1024,2,2,128]{0,3,2,1:T(8,128)(2,1)}, u32[]{:S(2)}) copy-start(bf16[1024,2,2,128]{0,3,2,1:T(8,128)(2,1)} %copy-done.1) | copy-start | bytes 3145732
Sparse Core Ops, SparseCore 0:
  10.1 127.1 all-gather.3
  207.2 56.8 all-gather.5
  267.6 64.3 reduce-scatter.4
  335.2 63.1 reduce-scatter.2
